TPU v7x, 128 devices: a whole 4x4x4 slice. The times are simulated.
128 devices in a mesh: row: 8 (over x, y_hi), col: 16 (over z, y_lo, core).
Axes of the slice: x: 4, y: 4 (y_hi: 2, y_lo: 2; y = y_hi * 2 + y_lo), z: 4, core: 2. Of those that a mesh axis runs over, the one named last changes fastest.
Arguments:
- density: float32 [5120, 5120], P('row', 'col'), as said below
- pattern: int32 [80, 80], P('row', 'col'), may hold values from 0 to 1, as said below
- weights: float32 [5120], P('row'), may hold values from 0.5 to 5
Outputs:
- purified: float32 [5120, 5120], P('row', 'col')
- checks: float32 [2, 5120], P(None, 'col')
Inputs may be any that keep to these rules, and one draw needn't show every extreme that they name: pattern is symmetric, and every block with |a - b| <= 2 is nonzero; the number of nonzero blocks differs strongly between block rows. density is symmetric and zero outside the blocks that pattern marks.
All inputs are finite; a program needn't handle non-finite values.
Results may differ from a plain program's by a relative error of at most 0.00012.
Values sent between devices are 32-bit elements; how exact they have to be, the bound alone decides.
A program may use at most 64 MiB of HBM per device.

v0:
```python
import jax
import jax.numpy as jnp
from jax import lax
from jax.sharding import PartitionSpec as P

BLK = 64


def full_dot(first, second):
    return jnp.dot(
        first, second, precision=lax.Precision.HIGHEST, preferred_element_type=jnp.float32
    )


def expand_mask(pattern):
    return jnp.repeat(jnp.repeat(pattern.astype(jnp.float32), BLK, axis=0), BLK, axis=1)


def multiply(left_tile, column, weight_row):
    partial_row = full_dot(weight_row, left_tile)
    result = full_dot(lax.all_gather(left_tile, "col", axis=1, tiled=True), column)
    summed = lax.psum(partial_row, "row")
    full_check = lax.all_gather(summed, "col", axis=1, tiled=True)
    check_row = full_dot(full_check, column)
    return (result, check_row)


def body(density, pattern, weights):
    block_mask = expand_mask(pattern)
    current = density
    weight_row = weights[None, :]
    checks = []
    column = lax.all_gather(current, "row", axis=0, tiled=True)
    square, first_check = multiply(current, column, weight_row)
    square = block_mask * square
    cube_term, second_check = multiply(square, column, weight_row)
    cube_term = block_mask * cube_term
    current = 3.0 * square - 2.0 * cube_term
    checks.append(first_check)
    checks.append(second_check)
    return (current, jnp.concatenate(checks, axis=0))


def solution(mesh):
    in_specs = (P("row", "col"), P("row", "col"), P("row"))
    out_specs = (P("row", "col"), P(None, "col"))
    return jax.shard_map(body, mesh=mesh, in_specs=in_specs, out_specs=out_specs, check_vma=False)
```

profile of v0, /device:TPU:1, one launch (start us, length us, event | category | flops | bytes accessed | tf_op | source)
XLA Modules:
  0.0 322.2 jit_solution(1333417447258999586)
XLA Ops:
  7.2 0.0 all-gather.6.cloned.1.call-start
  7.2 0.7 all-gather.6.cloned.1.call-update
  7.9 0.0 all-gather.4.cloned.1.call-start
  7.9 0.7 all-gather.4.cloned.1.call-update
  8.6 0.0 all-gather.8.cloned.1.call-start
  8.7 0.7 convert_element_type.3
  9.4 0.1 broadcast_in_dim.7
  9.5 0.1 reshape.24
  9.5 94.3 %all-gather.6.cloned.1.call-done = f32[5120,320]{0,1:T(8,128)} async-done(((f32[640,320]{0,1:T(8,128)}), f32[5120,320]{0,1:T(8,128)}) %all-gather.6.cloned.1.call-update) | async-done | bytes 6553616 | tf_op jit(solution)/shard_map/all_gather | solution.py:33
  103.8 75.1 %all-gather.4.cloned.1.call-done = f32[640,5120]{0,1:T(8,128)} async-done(((f32[640,320]{0,1:T(8,128)}), f32[640,5120]{0,1:T(8,128)}) %all-gather.4.cloned.1.call-update) | async-done | bytes 13107216 | tf_op jit(solution)/shard_map/all_gather | solution.py:21
  178.9 0.1 broadcast_in_dim.8
  179.0 0.0 copy-start.2
  179.0 0.0 copy-start.3
  179.0 0.0 copy-start.1
  179.0 20.3 %convolution_multiply_fusion.1 = f32[640,320]{0,1:T(8,128)} fusion(f32[640,320]{0,1:T(8,128)S(1)} %bitcast.18, f32[640,5120]{0,1:T(8,128)} %all-gather.4.cloned.1.call-done, f32[5120,320]{0,1:T(8,128)} %all-gather.6.cloned.1.call-done), kind=kOutput, calls=%fused_computation.1 | convolution fusion | flops 12583116800 | bytes 21299200 | tf_op jit(solution)/shard_map/dot_general | solution.py:10
  199.3 0.0 all-gather.8.cloned.1.call-update
  199.4 0.0 copy-done.2
  199.4 0.0 copy-done.3
  199.4 0.6 dynamic-slice
  200.7 0.0 copy-done.1
  200.7 0.8 fusion.2
  201.4 1.9 fusion.4
  203.3 20.8 %all-reduce.3 = (f32[1,320]{1,0:T(1,128)S(1)}, f32[1,320]{1,0:T(1,128)S(1)}) all-reduce(f32[1,320]{1,0:T(1,128)S(1)} %fusion.4, f32[1,320]{1,0:T(1,128)S(1)} %fusion.2), channel_id=1, replica_groups=mesh['row'=8,'col'=16] {'row'}, use_global_device_ids=true, to_apply=%region_1.0 | all-reduce | flops 640 | bytes 5120 | tf_op jit(solution)/shard_map/psum | solution.py:22
  224.2 0.3 dynamic-update-slice
  224.5 0.3 dynamic-update-slice.1
  224.7 55.3 %all-reduce.2 = (f32[5120]{0:T(1024)S(1)}, f32[5120]{0:T(1024)S(1)}) all-reduce(f32[5120]{0:T(1024)S(1)} %dynamic-update-slice.1, f32[5120]{0:T(1024)S(1)} %dynamic-update-slice), channel_id=1, replica_groups=mesh['row'=8,'col'=16] {'col'}, use_global_device_ids=true, to_apply=%add.1 | all-reduce | flops 10240 | bytes 81920 | tf_op jit(solution)/shard_map/reshape.10
  280.0 0.0 copy-start
  280.0 7.4 %fusion.3 = f32[1,320]{1,0:T(1,128)S(1)} fusion(f32[5120,1]{0,1:T(1,128)S(1)} %bitcast.21, f32[5120,320]{0,1:T(8,128)} %all-gather.6.cloned.1.call-done), kind=kOutput, calls=%fused_computation.6 | convolution fusion | flops 19660800 | bytes 6575360 | tf_op jit(solution)/shard_map/dot_general | solution.py:10
  287.4 7.3 %fusion.5 = f32[1,320]{1,0:T(1,128)S(1)} fusion(f32[5120,1]{0,1:T(1,128)S(1)} %bitcast.20, f32[5120,320]{0,1:T(8,128)} %all-gather.6.cloned.1.call-done), kind=kOutput, calls=%fused_computation.8 | convolution fusion | flops 19660800 | bytes 6575360 | tf_op jit(solution)/shard_map/dot_general | solution.py:10
  294.8 0.6 pad_maximum_fusion
  295.4 0.0 all-gather.8.cloned.1.call-done
  295.4 0.0 copy-done
  295.4 20.3 %fusion.1 = f32[640,320]{0,1:T(8,128)} fusion(f32[640,320]{0,1:T(8,128)S(1)} %bitcast.19, f32[640,5120]{0,1:T(8,128)} %all-gather.8.cloned.1.call-done, f32[5120,320]{0,1:T(8,128)} %all-gather.6.cloned.1.call-done, f32[640,320]{0,1:T(8,128)S(1)} %copy-done), kind=kOutput, calls=%fused_computation.3 | convolution fusion | flops 12583731200 | bytes 22118400 | tf_op jit(solution)/shard_map/dot_general | solution.py:10
  (5 shorter events, 0.1 us)
Async XLA Ops:
  7.2 96.7 %all-gather.6.cloned.1.call-start = ((), (), s32[]{:S(2)}) async-start(), calls=%async_computation.1 | async-start | bytes 7372800 | tf_op jit(solution)/shard_map/all_gather | solution.py:33
  7.9 171.0 %all-gather.4.cloned.1.call-start = ((), (), s32[]{:S(2)}) async-start(), calls=%async_computation | async-start | bytes 13926400 | tf_op jit(solution)/shard_map/all_gather | solution.py:21
  8.6 286.7 %all-gather.8.cloned.1.call-start = ((), (), s32[]{:S(2)}) async-start(), calls=%async_computation.2 | async-start | bytes 13926400 | tf_op jit(solution)/shard_map/all_gather | solution.py:21
  179.0 20.4 %copy-start.2 = (f32[640]{0:T(1024)S(1)}, f32[640]{0:T(1024)}, u32[]{:S(2)}) copy-start(f32[640]{0:T(1024)} %param.5) | copy-start | bytes 7684
  179.0 20.4 %copy-start.3 = (u32[128]{0:T(128)S(1)}, u32[128]{0:T(128)}, u32[]{:S(2)}) copy-start(u32[128]{0:T(128)} %constant.7) | copy-start | bytes 1540
  179.0 21.7 %copy-start.1 = (f32[640,320]{0,1:T(8,128)S(1)}, f32[640,320]{0,1:T(8,128)}, u32[]{:S(2)}) copy-start(f32[640,320]{0,1:T(8,128)} %param.3) | copy-start | bytes 2457604
  280.0 15.4 %copy-start = (f32[640,320]{0,1:T(8,128)S(1)}, f32[640,320]{0,1:T(8,128)}, u32[]{:S(2)}) copy-start(f32[640,320]{0,1:T(8,128)} %convolution_multiply_fusion.1) | copy-start | bytes 2457604
Sparse Core Ops, SparseCore 0:
  10.3 93.4 all-gather.5
  105.5 73.3 all-gather.3
  199.5 76.7 all-gather.7
where the time goes:
time: 325 us; the launch traced here: 322 us
  waiting for transfers between devices  171 us (53%)
  blocking collectives  76.1 us (23%)
  matrix products  58 us (18%)
  between operations  14.5 us (4%)
    all_gather x1, waiting for transfers between devices, body(): column = lax.all_gather(current, 'row', axis=0, tiled=True)  94.3 us
    all_gather x2, waiting for transfers between devices, multiply(): lax.all_gather(left_tile, 'col', axis=1, tiled=True)  75.1 us
    dot_general x6, matrix products, full_dot(): jnp.dot(first, second, precision=lax.Precision.HIGHEST, preferred_element...  58 us
    another operation x1, blocking collectives  55.3 us
    psum x1, blocking collectives, multiply(): summed = lax.psum(partial_row, 'row')  20.8 us
  transfers between devices with their start and end apart: 3, of which 2 were waited for; matrix products, arithmetic and copies ran while one was open for 6% of the time, Pallas kernels for 0%

commit v1 on v0

v1 whole, which is shorter than its diff:
```python
import jax
import jax.numpy as jnp
from jax import lax
from jax.experimental import pallas as pl
from jax.experimental.pallas import tpu as pltpu
from jax.sharding import PartitionSpec as P

BLK = 64
MESH = pl.DeviceIdType.MESH
ROWS, COLS = 640, 320
NROW, NCOL = 8, 16
HALF = COLS // 2
YQ = 64
SEMS = 112


def split(value):
    high = value.astype(jnp.bfloat16)
    low = (value - high.astype(jnp.float32)).astype(jnp.bfloat16)
    return high, low


def kernel(dens, pat, wts, out, chk, dcol, drow, srow, hop, acc, chk_out, chk_in, send, recv):
    row, col = lax.axis_index("row"), lax.axis_index("col")
    x, yh = row // 2, row % 2
    z, yl, core = col // 4, (col // 2) % 2, col % 2

    def dev(x_, yh_, z_, yl_, core_):
        return (x_ * 2 + yh_, (z_ * 2 + yl_) * 2 + core_)

    def step(value, by):
        return (value + by) % 4

    xp, xm = dev(step(x, 1), yh, z, yl, core), dev(step(x, 3), yh, z, yl, core)
    zp, zm = dev(x, yh, step(z, 1), yl, core), dev(x, yh, step(z, 3), yl, core)
    ya = dev(x, yh, z, 1 - yl, core)
    yb = dev(x, 1 - yh, z, 1 - yl, core)
    mate = dev(x, yh, z, yl, 1 - core)
    rows_of = [((row + i) % NROW, col) for i in range(1, NROW)]

    barrier = pltpu.get_barrier_semaphore()
    for peer in rows_of + [zp, zm, ya, yb, mate]:
        pl.semaphore_signal(barrier, inc=1, device_id=peer, device_id_type=MESH)

    tile = dens[...].T
    dcol[row] = tile
    drow[col] = tile
    rm = (lax.broadcasted_iota(jnp.int32, (NROW * 2, ROWS), 0)
          == lax.broadcasted_iota(jnp.int32, (NROW * 2, ROWS), 1) // BLK)
    cm = (lax.broadcasted_iota(jnp.int32, (COLS, 8), 1)
          == lax.broadcasted_iota(jnp.int32, (COLS, 8), 0) // BLK)
    nr, nc = ROWS // BLK, COLS // BLK
    pat_t = pat[...].astype(jnp.float32)
    part = lax.dot_general(cm[:, :nc].astype(jnp.float32), pat_t, (((1,), (1,)), ((), ())),
                           preferred_element_type=jnp.float32)
    mask = jnp.dot(part, rm[:nr].astype(jnp.float32), preferred_element_type=jnp.float32)

    pl.semaphore_wait(barrier, len(rows_of) + 5)

    copies = {}

    def put(name, src, dst, device):
        i = len(copies)
        copies[name] = pltpu.make_async_remote_copy(
            src_ref=src, dst_ref=dst, send_sem=send.at[i], recv_sem=recv.at[i],
            device_id=device, device_id_type=MESH)
        copies[name].start()

    def got(*names):
        for name in names:
            copies[name].wait_recv()

    def slot(z_, yl_, core_):
        return (z_ * 2 + yl_) * 2 + core_

    mine, mine_p = slot(z, yl, core), slot(z, 1 - yl, core)
    back, ahead, far = slot(step(z, 3), yl, core), slot(step(z, 1), yl, core), slot(step(z, 2), yl, core)
    back_p, ahead_p, far_p = (slot(step(z, 3), 1 - yl, core), slot(step(z, 1), 1 - yl, core),
                              slot(step(z, 2), 1 - yl, core))

    def half(buf, s, h):
        return buf.at[s, pl.ds(h * HALF, HALF), :]

    def same(name, ref, device):
        put(name, ref, ref, device)

    same("z+0", half(drow, mine, 0), zp)
    same("z-1", half(drow, mine, 1), zm)
    same("x+0", half(dcol, row, 0), xp)
    same("x-1", half(dcol, row, 1), xm)
    put("ya0", half(dcol, row, 0), hop.at[0], ya)
    put("yb1", half(dcol, row, 1), hop.at[1], yb)
    same("z+1", half(drow, mine, 1), zp)
    same("z-0", half(drow, mine, 0), zm)
    same("x+1", half(dcol, row, 1), xp)
    same("x-0", half(dcol, row, 0), xm)
    same("y0", half(drow, mine, 0), ya)
    same("c0", drow.at[mine], mate)

    def rowslot(x_, yh_):
        return x_ * 2 + yh_

    got("z+0")
    same("zz+", half(drow, back, 0), zp)
    got("z-1")
    same("zz-", half(drow, ahead, 1), zm)
    got("x+0")
    same("xx+", half(dcol, rowslot(step(x, 3), yh), 0), xp)
    got("x-1")
    same("xx-", half(dcol, rowslot(step(x, 1), yh), 1), xm)
    got("ya0")
    put("yab", hop.at[0], half(dcol, rowslot(x, yh), 0), yb)
    got("yb1")
    put("yba", hop.at[1], half(dcol, rowslot(x, 1 - yh), 1), ya)
    same("y1", half(drow, mine, 1), ya)
    rp = rowslot(x, 1 - yh)
    got("yab")
    same("xp+0", half(dcol, rp, 0), xp)
    same("xp-0", half(dcol, rp, 0), xm)
    got("y0")
    same("zp+0", half(drow, mine_p, 0), zp)
    same("zp-0", half(drow, mine_p, 0), zm)
    got("z+1")
    same("c1", drow.at[back], mate)
    got("z-0")
    same("c2", drow.at[ahead], mate)
    got("yba")
    same("xp+1", half(dcol, rp, 1), xp)
    same("xp-1", half(dcol, rp, 1), xm)
    got("zz+", "zz-")
    same("c3", drow.at[far], mate)
    got("y1")
    same("zp+1", half(drow, mine_p, 1), zp)
    same("zp-1", half(drow, mine_p, 1), zm)
    same("c4", drow.at[mine_p], mate)
    got("zp+0")
    same("zzp+", half(drow, back_p, 0), zp)
    got("xp+0")
    same("xxp+", half(dcol, rowslot(step(x, 3), 1 - yh), 0), xp)
    got("x+1", "x-0", "xx+", "xx-")
    got("zp-0", "zp-1")
    same("zzp-", half(drow, ahead_p, 1), zm)
    same("c6", drow.at[ahead_p], mate)
    got("xp-0", "xp-1")
    same("xxp-", half(dcol, rowslot(step(x, 1), 1 - yh), 1), xm)
    got("zp+1")
    same("c5", drow.at[back_p], mate)
    got("xp+1")
    got("c0", "c1", "c2", "c3", "c4", "c5", "c6")

    def product(panel, k):
        a_hi, a_lo = split(dcol[k])
        b_hi, b_lo = split(panel[pl.ds(2 * k, 2)].reshape(2 * COLS, ROWS))
        dot = lambda a, b: jnp.dot(a, b, preferred_element_type=jnp.float32)
        acc[...] += dot(a_hi, b_hi) + dot(a_hi, b_lo) + dot(a_lo, b_hi)

    def pick(i, values):
        k = values[-1]
        for j in reversed(range(len(values) - 1)):
            k = jnp.where(i == j, values[j], k)
        return k

    def products(panel, ks):
        if len(ks) == 1:
            product(panel, ks[0])
            return

        def run(i, carry):
            product(panel, pick(i, ks))
            return carry

        lax.fori_loop(0, len(ks), run, 0)

    d = (z - x + 4) % 4
    o0 = jnp.where(d == 2, step(x, 1), x)
    o1 = jnp.where(d <= 1, step(x, 1), step(x, 3))
    o2 = jnp.where(d == 0, step(x, 3), step(z, 2))
    o3 = step(x, 2)
    near, other = rowslot(o3, yh), rowslot(o2, 1 - yl)
    acc[...] = jnp.zeros_like(acc)
    products(drow, [rowslot(o0, yl), rowslot(o1, yl), rowslot(o0, 1 - yl), rowslot(o1, 1 - yl),
                    rowslot(o2, yl), jnp.where(d == 0, other, near)])
    got("zzp+", "zzp-")
    same("c7", drow.at[far_p], mate)
    got("xxp+", "xxp-")
    got("c7")
    products(drow, [jnp.where(d == 0, near, other), rowslot(o3, 1 - yh)])

    w8 = jnp.broadcast_to(wts[...], (8, ROWS))

    def column_sums(value):
        return lax.dot_general(w8, value, (((1,), (1,)), ((), ())),
                               precision=lax.Precision.HIGHEST, preferred_element_type=jnp.float32)

    square = acc[...]
    srow[col] = mask * square
    chk_out[0] = column_sums(square)

    def own(s, h):
        return srow.at[s, pl.ds(h * HALF, HALF), :]

    def late(s, h):
        return srow.at[s, pl.ds(h * HALF, YQ), :]

    def early(s, h):
        return srow.at[s, pl.ds(h * HALF + YQ, HALF - YQ), :]

    same("sz+0", own(mine, 0), zp)
    same("sz-1", own(mine, 1), zm)
    same("sy0", early(mine, 0), ya)
    same("sz+1", own(mine, 1), zp)
    same("sz-0", own(mine, 0), zm)
    same("sy1", early(mine, 1), ya)
    same("sc0", srow.at[mine], mate)
    same("sq0", late(mine, 0), ya)
    same("sq1", late(mine, 1), ya)
    for i in range(1, NROW):
        put(f"k{i}", chk_out.at[0], chk_in.at[0, row], rows_of[i - 1])
    acc[...] = jnp.zeros_like(acc)
    got("sc0")
    products(srow, [rowslot(z, yl)])
    got("sz+0")
    same("szz+", own(back, 0), zp)
    got("sz-1")
    same("szz-", own(ahead, 1), zm)
    got("sy0")
    same("szp+0", early(mine_p, 0), zp)
    same("szp-0", early(mine_p, 0), zm)
    got("sy1")
    same("szp-1", early(mine_p, 1), zm)
    same("szp+1", early(mine_p, 1), zp)
    got("sz+1")
    same("sq2", late(back, 0), ya)
    same("sq3", late(back, 1), ya)
    same("sc1", srow.at[back], mate)
    got("sz-0")
    same("sq4", late(ahead, 0), ya)
    same("sq5", late(ahead, 1), ya)
    same("sc2", srow.at[ahead], mate)
    got("sq0", "sq1")
    same("sc4", srow.at[mine_p], mate)
    got("sc1", "sc2")
    products(srow, [rowslot(step(z, 3), yl), rowslot(step(z, 1), yl)])
    got("szz+", "szz-")
    same("sq6", late(far, 0), ya)
    same("sq7", late(far, 1), ya)
    same("sc3", srow.at[far], mate)
    got("szp+0")
    same("szzp+", early(back_p, 0), zp)
    got("szp-0", "szp-1")
    same("szzp-", early(ahead_p, 1), zm)
    got("sq4", "sq5")
    same("sc6", srow.at[ahead_p], mate)
    got("szp+1", "sq2", "sq3")
    same("sc5", srow.at[back_p], mate)
    got("sc3", "sc4", "sc5", "sc6")
    products(srow, [rowslot(step(z, 2), yl), rowslot(z, 1 - yl), rowslot(step(z, 1), 1 - yl),
                    rowslot(step(z, 3), 1 - yl)])
    got("szzp+", "szzp-", "sq6", "sq7")
    same("sc7", srow.at[far_p], mate)
    got("sc7")
    products(srow, [rowslot(step(z, 2), 1 - yl)])

    cube = acc[...]
    chk_out[1] = column_sums(cube)
    for i in range(1, NROW):
        put(f"l{i}", chk_out.at[1], chk_in.at[1, row], rows_of[i - 1])
    chk_in[0, row] = chk_out[0]
    chk_in[1, row] = chk_out[1]
    out[...] = (3.0 * srow[col] - 2.0 * (mask * cube)).T
    for i in range(1, NROW):
        got(f"k{i}", f"l{i}")
    total0, total1 = chk_in[0, 0], chk_in[1, 0]
    for i in range(1, NROW):
        total0 += chk_in[0, i]
        total1 += chk_in[1, i]
    chk[...] = jnp.concatenate([total0[:1], total1[:1]], axis=0)
    for copy in copies.values():
        copy.wait_send()
    assert len(copies) <= SEMS


def body(density, pattern, weights):
    f32 = jnp.float32
    vmem = pl.BlockSpec(memory_space=pltpu.VMEM)
    return pl.pallas_call(
        kernel,
        out_shape=(jax.ShapeDtypeStruct((ROWS, COLS), f32), jax.ShapeDtypeStruct((2, COLS), f32)),
        in_specs=[vmem] * 3,
        out_specs=(vmem, vmem),
        scratch_shapes=[
            pltpu.VMEM((NROW, COLS, ROWS), f32),
            pltpu.VMEM((NCOL, COLS, ROWS), f32),
            pltpu.VMEM((NCOL, COLS, ROWS), f32),
            pltpu.VMEM((2, HALF, ROWS), f32),
            pltpu.VMEM((COLS, ROWS), f32),
            pltpu.VMEM((2, 8, COLS), f32),
            pltpu.VMEM((2, NROW, 8, COLS), f32),
            pltpu.SemaphoreType.DMA((SEMS,)),
            pltpu.SemaphoreType.DMA((SEMS,)),
        ],
        compiler_params=pltpu.CompilerParams(
            collective_id=0, has_side_effects=True, vmem_limit_bytes=63 * 1024 * 1024),
        name="purify",
    )(density, pattern, weights[None, :])


def solution(mesh):
    in_specs = (P("row", "col"), P("row", "col"), P("row"))
    out_specs = (P("row", "col"), P(None, "col"))
    return jax.shard_map(body, mesh=mesh, in_specs=in_specs, out_specs=out_specs, check_vma=False)
```

time: 325 us -> 141 us (0.43)
  waiting for transfers between devices: 171 us -> 0 us
  Pallas kernels: 0 us -> 131 us
  blocking collectives: 76.1 us -> 0 us
  matrix products: 58 us -> 0 us
  between operations: 14.5 us -> 0.66 us
  local copies, waits for them, and re-layouts: 1.36 us -> 7.41 us
    all_gather x3 -> x0, waiting for transfers between devices: 169 us -> none  [the longest x1 94.3 us: body(): column = lax.all_gather(current, 'row', axis=0, tiled=True)]
    pallas_call x0 -> x1, Pallas kernels: none -> 131 us  [body(): pl.pallas_call(kernel, out_shape=(jax.ShapeDtypeStruct((ROWS, COLS), f32)...]
    dot_general x6 -> x0, matrix products: 58 us -> none  [full_dot(): jnp.dot(first, second, precision=lax.Precision.HIGHEST, preferred_element...]
    another operation x1 -> x0, blocking collectives: 55.3 us -> none
    psum x1 -> x0, blocking collectives: 20.8 us -> none  [multiply(): summed = lax.psum(partial_row, 'row')]
  transfers between devices with their start and end apart: 3 -> 0, of which waited for: 2 -> 0; matrix products, arithmetic and copies ran while one was open for 6% -> 0% of each run, Pallas kernels for 0% -> 0%
where the time goes in v1:
time: 141 us; the launch traced here: 139 us
  Pallas kernels  131 us (93%)
  local copies, waits for them, and re-layouts  7.41 us (5%)
    pallas_call x1, Pallas kernels, body(): pl.pallas_call(kernel, out_shape=(jax.ShapeDtypeStruct((ROWS, COLS), f32)...  131 us
    unnamed x7, local copies, waits for them, and re-layouts  3.72 us

profile of v1, /device:TPU:1, one launch (start us, length us, event | category | flops | bytes accessed | tf_op | source)
XLA Modules:
  0.0 138.9 jit_solution(1019146579422797691)
XLA Ops:
  0.6 0.0 copy-start
  0.6 1.3 broadcast_in_dim.3.wts
  1.9 0.0 copy-done
  1.9 0.7 copy.6.pat
  2.6 2.5 %copy.5.dens = f32[640,320]{1,0:T(8,128)} copy(f32[640,320]{0,1:T(8,128)} %param.3) | data formatting | bytes 1638400 | tf_op args[0]
  5.1 130.8 %purify.1 = (f32[640,320]{1,0:T(8,128)}, f32[2,320]{1,0:T(2,128)}) custom-call(f32[640,320]{1,0:T(8,128)} %copy.5.dens, s32[10,5]{1,0:T(8,128)} %copy.6.pat, f32[1,640]{1,0:T(1,128)} %broadcast_in_dim.3.wts), custom_call_target="tpu_custom_call" | custom-call | tf_op jit(solution)/shard_map/purify/pallas_call | solution.py:286
  135.9 0.0 copy-start.1
  135.9 2.4 %copy.7 = f32[640,320]{0,1:T(8,128)} copy(f32[640,320]{1,0:T(8,128)} %get-tuple-element.2) | data formatting | bytes 1638400 | tf_op jit(solution)/shard_map/purify/pallas_call | solution.py:286
  138.3 0.0 copy-done.1
  138.3 0.6 copy.9
Async XLA Ops:
  0.6 1.3 copy-start
  135.9 2.4 %copy-start.1 = (f32[2,320]{1,0:T(2,128)S(1)}, f32[2,320]{1,0:T(2,128)}, u32[]{:S(2)}) copy-start(f32[2,320]{1,0:T(2,128)} %get-tuple-element.7) | copy-start | bytes 7684

commit v2 on v1

--- a/solution.py
+++ b/solution.py
@@ -42,7 +42,7 @@
     for peer in rows_of + [zp, zm, ya, yb, mate]:
         pl.semaphore_signal(barrier, inc=1, device_id=peer, device_id_type=MESH)
 
-    tile = dens[...].T
+    tile = dens[...]
     dcol[row] = tile
     drow[col] = tile
     rm = (lax.broadcasted_iota(jnp.int32, (NROW * 2, ROWS), 0)
@@ -50,9 +50,8 @@
     cm = (lax.broadcasted_iota(jnp.int32, (COLS, 8), 1)
           == lax.broadcasted_iota(jnp.int32, (COLS, 8), 0) // BLK)
     nr, nc = ROWS // BLK, COLS // BLK
-    pat_t = pat[...].astype(jnp.float32)
-    part = lax.dot_general(cm[:, :nc].astype(jnp.float32), pat_t, (((1,), (1,)), ((), ())),
-                           preferred_element_type=jnp.float32)
+    part = jnp.dot(cm[:, :nc].astype(jnp.float32), pat[...].astype(jnp.float32),
+                   preferred_element_type=jnp.float32)
     mask = jnp.dot(part, rm[:nr].astype(jnp.float32), preferred_element_type=jnp.float32)
 
     pl.semaphore_wait(barrier, len(rows_of) + 5)
@@ -186,7 +185,7 @@
     got("c7")
     products(drow, [jnp.where(d == 0, near, other), rowslot(o3, 1 - yh)])
 
-    w8 = jnp.broadcast_to(wts[...], (8, ROWS))
+    w8 = jnp.broadcast_to(wts[...][None, :], (8, ROWS))
 
     def column_sums(value):
         return lax.dot_general(w8, value, (((1,), (1,)), ((), ())),
@@ -267,7 +266,7 @@
         put(f"l{i}", chk_out.at[1], chk_in.at[1, row], rows_of[i - 1])
     chk_in[0, row] = chk_out[0]
     chk_in[1, row] = chk_out[1]
-    out[...] = (3.0 * srow[col] - 2.0 * (mask * cube)).T
+    out[...] = 3.0 * srow[col] - 2.0 * (mask * cube)
     for i in range(1, NROW):
         got(f"k{i}", f"l{i}")
     total0, total1 = chk_in[0, 0], chk_in[1, 0]
@@ -283,9 +282,9 @@
 def body(density, pattern, weights):
     f32 = jnp.float32
     vmem = pl.BlockSpec(memory_space=pltpu.VMEM)
-    return pl.pallas_call(
+    purified, checks = pl.pallas_call(
         kernel,
-        out_shape=(jax.ShapeDtypeStruct((ROWS, COLS), f32), jax.ShapeDtypeStruct((2, COLS), f32)),
+        out_shape=(jax.ShapeDtypeStruct((COLS, ROWS), f32), jax.ShapeDtypeStruct((2, COLS), f32)),
         in_specs=[vmem] * 3,
         out_specs=(vmem, vmem),
         scratch_shapes=[
@@ -302,7 +301,8 @@
         compiler_params=pltpu.CompilerParams(
             collective_id=0, has_side_effects=True, vmem_limit_bytes=63 * 1024 * 1024),
         name="purify",
-    )(density, pattern, weights[None, :])
+    )(density.T, pattern.T, weights)
+    return purified.T, checks
 
 
 def solution(mesh):

time: 141 us -> 136 us (0.965)
  local copies, waits for them, and re-layouts: 7.41 us -> 2.67 us
    pallas_call x1 -> x0, local copies, waits for them, and re-layouts: 2.41 us -> none  [body(): pl.pallas_call(kernel, out_shape=(jax.ShapeDtypeStruct((ROWS, COLS), f32)...]
    unnamed x7 -> x4, local copies, waits for them, and re-layouts: 3.72 us -> 2.67 us
where the time goes in v2:
time: 136 us; the launch traced here: 134 us
  Pallas kernels  131 us (96%)
  local copies, waits for them, and re-layouts  2.67 us (2%)
    pallas_call x1, Pallas kernels, body(): pl.pallas_call(kernel, out_shape=(jax.ShapeDtypeStruct((COLS, ROWS), f32)...  131 us

profile of v2, /device:TPU:1, one launch (start us, length us, event | category | flops | bytes accessed | tf_op | source)
XLA Modules:
  0.0 134.0 jit_solution(13850927996964257792)
XLA Ops:
  0.6 130.7 %purify.1 = (f32[320,640]{1,0:T(8,128)}, f32[2,320]{1,0:T(2,128)}) custom-call(f32[320,640]{1,0:T(8,128)} %bitcast.3, s32[5,10]{1,0:T(8,128)} %bitcast.5, f32[640]{0:T(1024)} %wts.1), custom_call_target="tpu_custom_call" | custom-call | tf_op jit(solution)/shard_map/purify/pallas_call | solution.py:285
  131.3 0.0 copy-start
  131.4 2.1 %copy.7 = f32[640,320]{0,1:T(8,128)} copy(f32[640,320]{0,1:T(8,128)} %bitcast.4) | data formatting | bytes 1638400
  133.4 0.0 copy-done
  133.5 0.6 copy.8
Async XLA Ops:
  131.3 2.1 %copy-start = (f32[2,320]{1,0:T(2,128)S(1)}, f32[2,320]{1,0:T(2,128)}, u32[]{:S(2)}) copy-start(f32[2,320]{1,0:T(2,128)} %get-tuple-element.9) | copy-start | bytes 7684

commit v3 on v0

v3 whole, which is shorter than its diff:
```python
import jax
import jax.numpy as jnp
from jax import lax
from jax.experimental import pallas as pl
from jax.experimental.pallas import tpu as pltpu
from jax.sharding import PartitionSpec as P

BLK = 64
MESH = pl.DeviceIdType.MESH
ROWS, COLS = 640, 320
NROW, NCOL = 8, 16
SEMS = 240

LINK_ROW, LINK_LATENCY = 0.0545, 1.7
MATE_ROW, MATE_LATENCY = 0.0057, 1.0
LEAD = 3.0

PIECES_D = ((0, 80, "first", 1), (80, 80, "first", 1), (160, 80, "first", -1), (240, 80, "first", -1))
PIECES_S = ((0, 88, "first", 1), (88, 72, "after", 1), (160, 88, "first", -1), (248, 72, "after", -1))
GROUPS = ((0, 160), (160, 160))


class Plan:
    def __init__(self):
        self.items, self.made = {}, {}

    def add(self, name, link, rows, deps, do):
        if link == "work":
            length, latency = rows, 0.0
        elif link == "mate":
            length, latency = rows * MATE_ROW, MATE_LATENCY
        else:
            length, latency = rows * LINK_ROW, LINK_LATENCY
        self.items[name] = (link, length, latency, tuple(deps), do)

    def order(self):
        items = self.items
        after = {name: [] for name in items}
        for name, item in items.items():
            for dep in item[3]:
                after[dep].append(name)
        level = {}
        for name in reversed(list(items)):
            _, length, latency, _, _ = items[name]
            level[name] = length + latency + max([level[n] for n in after[name]], default=0.0)
        free, there, events = {}, {}, []
        left = list(items)
        while left:
            best = None
            for name in left:
                link, _, _, deps, _ = items[name]
                if all(dep in there for dep in deps):
                    ready = max([there[dep] for dep in deps], default=0.0)
                    key = (max(ready, free.get(link, 0.0)), -level[name], len(events))
                    if best is None or key < best[0]:
                        best = (key, name, ready)
            (start, _, _), name, ready = best
            link, length, latency, _, _ = items[name]
            free[link] = start + length
            there[name] = start + length + latency
            issue = start if link == "work" else max(ready, start - LEAD)
            events.append((issue, len(events), name))
            left.remove(name)
        return [name for _, _, name in sorted(events)], there

    def run(self, wait):
        done = set()
        for name in self.order()[0]:
            _, _, _, deps, do = self.items[name]
            for dep in deps:
                if dep not in done and self.items[dep][0] != "work":
                    wait(dep)
                    done.add(dep)
            do(name)
        for name in self.items:
            if name not in done and self.items[name][0] != "work":
                wait(name)


def ring(plan, tag, pieces, plus, minus, cross, send_to):
    fills = {slot: {} for slot in ("back", "ahead", "far", "mine_p", "back_p", "ahead_p", "far_p")}

    def over(name, src, dst, p, deps):
        first, rows = pieces[p][:2]
        last = deps
        for i, link in enumerate(cross(p)):
            step = f"{name}/{i}"
            plan.add(step, link, rows, last, send_to(step, link, src, dst, first, rows, i, p))
            last = [step]
        fills[dst][p] = last[0]
        return last

    def around(kind, p, deps, slots):
        mine, back, ahead, far = slots
        first, rows, _, way = pieces[p]
        names = {}
        for link, dst in ((plus, back), (minus, ahead)):
            name = f"{tag}{kind}{link}{p}"
            plan.add(name, link, rows, deps, send_to(name, link, mine, dst, first, rows, 0, p))
            fills[dst][p] = name
            names[link] = name
        link, src = (plus, back) if way > 0 else (minus, ahead)
        name = f"{tag}{kind}far{p}"
        plan.add(name, link, rows, [names[link]], send_to(name, link, src, far, first, rows, 0, p))
        fills[far][p] = name

    for p, (first, rows, when, way) in enumerate(pieces):
        around("own", p, [], ("mine", "back", "ahead", "far"))
        if when == "first":
            last = over(f"{tag}y{p}", "mine", "mine_p", p, [])
            around("par", p, last, ("mine_p", "back_p", "ahead_p", "far_p"))
        else:
            over(f"{tag}y{p}", "mine", "mine_p", p, [])
            for slot in ("back", "ahead", "far"):
                over(f"{tag}y{slot}{p}", slot, slot + "_p", p, [fills[slot][p]])
    return fills


def split(value):
    high = value.astype(jnp.bfloat16)
    low = (value - high.astype(jnp.float32)).astype(jnp.bfloat16)
    return high, low


def dot3(a, b):
    (a_hi, a_lo), (b_hi, b_lo) = split(a), split(b)
    dot = lambda u, v: jnp.dot(u, v, preferred_element_type=jnp.float32)
    return dot(a_hi, b_hi) + dot(a_hi, b_lo) + dot(a_lo, b_hi)


def kernel(dens, pat, wts, out, chk, dcol, drow, srow, hop, acc,
           sums_out, sums_in, parts_out, parts_in, send, recv):
    row, col = lax.axis_index("row"), lax.axis_index("col")
    x, yh = row // 2, row % 2
    z, yl, core = col // 4, (col // 2) % 2, col % 2

    def dev(x_, yh_, z_, yl_, core_):
        return (x_ * 2 + yh_, (z_ * 2 + yl_) * 2 + core_)

    def step(value, by):
        return (value + by) % 4

    def rowslot(x_, yh_):
        return x_ * 2 + yh_

    def colslot(z_, yl_):
        return (z_ * 2 + yl_) * 2 + core

    peer = {
        "x+": dev(step(x, 1), yh, z, yl, core), "x-": dev(step(x, 3), yh, z, yl, core),
        "z+": dev(x, yh, step(z, 1), yl, core), "z-": dev(x, yh, step(z, 3), yl, core),
        "ya": dev(x, yh, z, 1 - yl, core), "yb": dev(x, 1 - yh, z, 1 - yl, core),
        "mate": dev(x, yh, z, yl, 1 - core),
    }
    rows_of = [((row + i) % NROW, col) for i in range(1, NROW)]
    cols_of = [(row, (col + i) % NCOL) for i in range(1, NCOL)]

    barrier = pltpu.get_barrier_semaphore()
    greet = rows_of + cols_of + [peer["yb"]]
    for device in greet:
        pl.semaphore_signal(barrier, inc=1, device_id=device, device_id_type=MESH)

    tile = dens[...]
    dcol[row] = tile
    drow[col] = tile
    acc[...] = jnp.zeros_like(acc)
    nr, nc = ROWS // BLK, COLS // BLK
    rm = (lax.broadcasted_iota(jnp.int32, (nr, ROWS), 0)
          == lax.broadcasted_iota(jnp.int32, (nr, ROWS), 1) // BLK)
    cm = (lax.broadcasted_iota(jnp.int32, (COLS, nc), 1)
          == lax.broadcasted_iota(jnp.int32, (COLS, nc), 0) // BLK)
    part = jnp.dot(cm.astype(jnp.float32), pat[...].astype(jnp.float32),
                   preferred_element_type=jnp.float32)
    mask = jnp.dot(part, rm.astype(jnp.float32), preferred_element_type=jnp.float32)

    pl.semaphore_wait(barrier, len(greet))

    copies = {}

    def put(name, src, dst, device):
        i = len(copies)
        copies[name] = pltpu.make_async_remote_copy(
            src_ref=src, dst_ref=dst, send_sem=send.at[i], recv_sem=recv.at[i],
            device_id=device, device_id_type=MESH)
        copies[name].start()

    def wait(name):
        copies[name].wait_recv()

    rowslots = {
        "mine": row, "back": rowslot(step(x, 3), yh), "ahead": rowslot(step(x, 1), yh),
        "far": rowslot(step(x, 2), yh), "mine_p": rowslot(x, 1 - yh),
        "back_p": rowslot(step(x, 3), 1 - yh), "ahead_p": rowslot(step(x, 1), 1 - yh),
        "far_p": rowslot(step(x, 2), 1 - yh),
    }
    colslots = {
        "mine": col, "back": colslot(step(z, 3), yl), "ahead": colslot(step(z, 1), yl),
        "far": colslot(step(z, 2), yl), "mine_p": colslot(z, 1 - yl),
        "back_p": colslot(step(z, 3), 1 - yl), "ahead_p": colslot(step(z, 1), 1 - yl),
        "far_p": colslot(step(z, 2), 1 - yl),
    }

    def panel_copy(buf, slots):
        def make(name, link, src, dst, first, rows, i, p):
            ref = buf.at[slots[src], pl.ds(first, rows), :]
            return lambda _: put(name, ref, ref, peer[link])
        return make

    def column_copy(name, link, src, dst, first, rows, i, p):
        span = pl.ds(first, rows)
        here = dcol.at[rowslots[src], span, :]
        if link in ("x+", "x-"):
            return lambda _: put(name, here, here, peer[link])
        place = ("mine", "back", "ahead", "far").index(src)
        between = hop.at[place, span, :]
        if i == 0:
            return lambda _: put(name, here, between, peer[link])
        origin = rowslot(step(x, (0, 3, 1, 2)[place]), yh if link == "yb" else 1 - yh)
        there = dcol.at[origin, span, :]
        return lambda _: put(name, between, there, peer[link])

    def mates(plan, tag, buf, fills, pieces):
        given = {"mine": []}
        name = f"{tag}m"
        ref = buf.at[col]
        plan.add(name, "mate", COLS, [], lambda _, n=name, r=ref: put(n, r, r, peer["mate"]))
        given["mine"].append(name)
        for slot, by in fills.items():
            given[slot] = []
            groups = [q[:2] for q in pieces] if slot == "far_p" else GROUPS
            for first, rows in groups:
                deps = [by[p] for p, q in enumerate(pieces) if first <= q[0] < first + rows]
                name = f"{tag}m{slot}{first}"
                ref = buf.at[colslots[slot], pl.ds(first, rows), :]
                plan.add(name, "mate", rows, deps, lambda _, n=name, r=ref: put(n, r, r, peer["mate"]))
                given[slot].append(name)
        return {slot: list(by.values()) + given[slot] for slot, by in fills.items()} | {"mine": given["mine"]}

    def product(panel, k):
        acc[...] += dot3(dcol[k], panel[pl.ds(2 * k, 2)].reshape(2 * COLS, ROWS))

    def pick(i, values):
        k = values[-1]
        for j in reversed(range(len(values) - 1)):
            k = jnp.where(i == j, values[j], k)
        return k

    def products(panel, ks):
        def do(_):
            if len(ks) == 1:
                product(panel, ks[0])
                return

            def run(i, carry):
                product(panel, pick(i, ks))
                return carry

            lax.fori_loop(0, len(ks), run, 0)
        return do

    plan = Plan()
    fill_c = ring(plan, "C", PIECES_D, "x+", "x-",
                  lambda p: ("ya", "yb") if PIECES_D[p][3] > 0 else ("yb", "ya"), column_copy)
    fill_r = ring(plan, "R", PIECES_D, "z+", "z-", lambda p: ("ya",), panel_copy(drow, colslots))
    have = mates(plan, "R", drow, fill_r, PIECES_D)

    def need(r_slots, c_slots):
        return ([n for s in r_slots for n in have[s]] + [n for s in c_slots for n in fill_c[s].values()])

    d, even = (z - x + 4) % 4, yl == yh
    ny = 1 - yl
    o0 = jnp.where(d == 2, step(x, 1), x)
    o1 = jnp.where(d <= 1, step(x, 1), step(x, 3))
    o2 = jnp.where(d == 0, step(x, 3), step(z, 2))
    o3 = step(x, 2)
    sel = lambda a, b: jnp.where(even, a, b)
    stage1 = [rowslot(x, yl), sel(rowslot(step(x, 1), yl), rowslot(z, yh))]
    stage2 = [sel(rowslot(step(x, 2), yl), rowslot(step(x, 1), yl)), rowslot(step(x, 3), yl),
              sel(rowslot(o0, ny), rowslot(step(z, 1), yh)), sel(rowslot(o1, ny), rowslot(step(z, 3), yh))]
    stage3 = [sel(rowslot(o2, ny), rowslot(step(x, 2), yl)), sel(rowslot(o3, ny), rowslot(step(z, 2), yh))]
    near = ["back", "ahead", "far", "mine_p"]
    plan.add("work1", "work", 2.6, need(["mine"] + near, near), products(drow, stage1))
    near2 = near + ["back_p", "ahead_p"]
    plan.add("work2", "work", 5.2, need(near2, near2) + ["work1"], products(drow, stage2))
    near3 = near2 + ["far_p"]
    plan.add("work3", "work", 2.6, need(near3, near3) + ["work2"], products(drow, stage3))
    plan.run(wait)

    w8 = jnp.broadcast_to(wts[...][None, :], (8, ROWS))

    def column_sums(value):
        return lax.dot_general(w8, value, (((1,), (1,)), ((), ())),
                               precision=lax.Precision.HIGHEST, preferred_element_type=jnp.float32)

    srow[col] = mask * acc[...]

    plan = Plan()
    fill_s = ring(plan, "S", PIECES_S, "z+", "z-", lambda p: ("ya",), panel_copy(srow, colslots))
    have = mates(plan, "S", srow, fill_s, PIECES_S)

    def sums(_):
        first = lax.broadcasted_iota(jnp.int32, (8, COLS), 0) == 0
        value = jnp.where(first, column_sums(acc[...]), column_sums(srow[col]))
        acc[...] = jnp.zeros_like(acc)
        sums_out[...] = value
        sums_in[row] = value
        for i, device in enumerate(rows_of):
            put(f"sums{i}", sums_out, sums_in.at[row], device)

    def parts(_):
        for i in range(NROW - 1):
            wait(f"sums{i}")
        total = sums_in[0]
        for i in range(1, NROW):
            total += sums_in[i]
        chk[0:1, :] = total[0:1]

        def run(k, carry):
            value = dot3(total, dcol[k])
            parts_out[2 * k] = value[:, :COLS]
            parts_out[2 * k + 1] = value[:, COLS:]
            return carry

        lax.fori_loop(0, NROW, run, 0)
        parts_in[col] = parts_out[col]
        for i, device in enumerate(cols_of):
            put(f"parts{i}", parts_out.at[device[1]], parts_in.at[col], device)

    plan.add("sums", "work", 2.5, [], sums)
    plan.add("work0", "work", 1.3, have["mine"] + ["sums"], products(srow, [rowslot(z, yl)]))
    plan.add("parts", "work", 6.0, fill_s["far"].values(), parts)
    plan.add("work1", "work", 2.6, have["back"] + have["ahead"] + ["work0"],
             products(srow, [rowslot(step(z, 3), yl), rowslot(step(z, 1), yl)]))
    plan.add("work2", "work", 2.6, have["far"] + have["mine_p"] + ["work1"],
             products(srow, [rowslot(step(z, 2), yl), rowslot(z, 1 - yl)]))
    plan.add("work3", "work", 2.6, have["back_p"] + have["ahead_p"] + ["work2"],
             products(srow, [rowslot(step(z, 3), 1 - yl), rowslot(step(z, 1), 1 - yl)]))
    plan.add("work4", "work", 1.3, have["far_p"] + ["work3"],
             products(srow, [rowslot(step(z, 2), 1 - yl)]))
    plan.run(wait)

    out[...] = 3.0 * srow[col] - 2.0 * (mask * acc[...])
    for i in range(NCOL - 1):
        wait(f"parts{i}")
    total = parts_in[0]
    for i in range(1, NCOL):
        total += parts_in[i]
    chk[1:2, :] = total[1:2]
    for copy in copies.values():
        copy.wait_send()
    assert len(copies) <= SEMS, len(copies)


def body(density, pattern, weights):
    f32 = jnp.float32
    vmem = pl.BlockSpec(memory_space=pltpu.VMEM)
    purified, checks = pl.pallas_call(
        kernel,
        out_shape=(jax.ShapeDtypeStruct((COLS, ROWS), f32), jax.ShapeDtypeStruct((2, COLS), f32)),
        in_specs=[vmem] * 3,
        out_specs=(vmem, vmem),
        scratch_shapes=[
            pltpu.VMEM((NROW, COLS, ROWS), f32),
            pltpu.VMEM((NCOL, COLS, ROWS), f32),
            pltpu.VMEM((NCOL, COLS, ROWS), f32),
            pltpu.VMEM((4, COLS, ROWS), f32),
            pltpu.VMEM((COLS, ROWS), f32),
            pltpu.VMEM((8, COLS), f32),
            pltpu.VMEM((NROW, 8, COLS), f32),
            pltpu.VMEM((NCOL, 8, COLS), f32),
            pltpu.VMEM((NCOL, 8, COLS), f32),
            pltpu.SemaphoreType.DMA((SEMS,)),
            pltpu.SemaphoreType.DMA((SEMS,)),
        ],
        compiler_params=pltpu.CompilerParams(
            collective_id=0, has_side_effects=True, vmem_limit_bytes=63 * 1024 * 1024),
        name="purify",
    )(density.T, pattern.T, weights)
    return purified.T, checks


def solution(mesh):
    in_specs = (P("row", "col"), P("row", "col"), P("row"))
    out_specs = (P("row", "col"), P(None, "col"))
    return jax.shard_map(body, mesh=mesh, in_specs=in_specs, out_specs=out_specs, check_vma=False)
```

time: 325 us -> 129 us (0.40)
  waiting for transfers between devices: 171 us -> 0 us
  Pallas kernels: 0 us -> 125 us
  blocking collectives: 76.1 us -> 0 us
  matrix products: 58 us -> 0 us
  between operations: 14.5 us -> 0.65 us
    all_gather x3 -> x0, waiting for transfers between devices: 169 us -> none  [the longest x1 94.3 us: body(): column = lax.all_gather(current, 'row', axis=0, tiled=True)]
    pallas_call x0 -> x1, Pallas kernels: none -> 125 us  [body(): pl.pallas_call(kernel, out_shape=(jax.ShapeDtypeStruct((COLS, ROWS), f32)...]
    dot_general x6 -> x0, matrix products: 58 us -> none  [full_dot(): jnp.dot(first, second, precision=lax.Precision.HIGHEST, preferred_element...]
    another operation x1 -> x0, blocking collectives: 55.3 us -> none
    psum x1 -> x0, blocking collectives: 20.8 us -> none  [multiply(): summed = lax.psum(partial_row, 'row')]
  transfers between devices with their start and end apart: 3 -> 0, of which waited for: 2 -> 0; matrix products, arithmetic and copies ran while one was open for 6% -> 0% of each run, Pallas kernels for 0% -> 0%
where the time goes in v3:
time: 129 us
  Pallas kernels  125 us (97%)
  local copies, waits for them, and re-layouts  2.67 us (2%)
    pallas_call x1, Pallas kernels, body(): pl.pallas_call(kernel, out_shape=(jax.ShapeDtypeStruct((COLS, ROWS), f32)...  125 us
    unnamed x4, local copies, waits for them, and re-layouts  2.67 us

profile of v3, /device:TPU:1, one launch (start us, length us, event | category | flops | bytes accessed | tf_op | source)
XLA Modules:
  0.0 128.6 jit_solution(7334082078197601471)
XLA Ops:
  0.6 125.3 %purify.1 = (f32[320,640]{1,0:T(8,128)}, f32[2,320]{1,0:T(2,128)}) custom-call(f32[320,640]{1,0:T(8,128)} %bitcast.3, s32[5,10]{1,0:T(8,128)} %bitcast.5, f32[640]{0:T(1024)} %wts.1), custom_call_target="tpu_custom_call" | custom-call | tf_op jit(solution)/shard_map/purify/pallas_call | solution.py:357
  125.9 0.0 copy-start
  126.0 2.1 %copy.7 = f32[640,320]{0,1:T(8,128)} copy(f32[640,320]{0,1:T(8,128)} %bitcast.4) | data formatting | bytes 1638400
  128.0 0.0 copy-done
  128.0 0.6 copy.8
Async XLA Ops:
  125.9 2.1 %copy-start = (f32[2,320]{1,0:T(2,128)S(1)}, f32[2,320]{1,0:T(2,128)}, u32[]{:S(2)}) copy-start(f32[2,320]{1,0:T(2,128)} %get-tuple-element.9) | copy-start | bytes 7684

commit v4 on v3

--- a/solution.py
+++ b/solution.py
@@ -13,9 +13,12 @@
 
 LINK_ROW, LINK_LATENCY = 0.0545, 1.7
 MATE_ROW, MATE_LATENCY = 0.0057, 1.0
-LEAD = 3.0
-
-PIECES_D = ((0, 80, "first", 1), (80, 80, "first", 1), (160, 80, "first", -1), (240, 80, "first", -1))
+LEAD = 5.0
+
+PIECES_C = ((0, 72, "first", 1), (72, 72, "first", 1), (144, 16, "after", 1),
+            (160, 72, "first", -1), (232, 72, "first", -1), (304, 16, "after", -1))
+PIECES_R = ((0, 64, "first", 1), (64, 72, "first", 1), (136, 24, "after", 1),
+            (160, 64, "first", -1), (224, 72, "first", -1), (296, 24, "after", -1))
 PIECES_S = ((0, 88, "first", 1), (88, 72, "after", 1), (160, 88, "first", -1), (248, 72, "after", -1))
 GROUPS = ((0, 160), (160, 160))
 
@@ -128,8 +131,8 @@
     return dot(a_hi, b_hi) + dot(a_hi, b_lo) + dot(a_lo, b_hi)
 
 
-def kernel(dens, pat, wts, out, chk, dcol, drow, srow, hop, acc,
-           sums_out, sums_in, parts_out, parts_in, send, recv):
+def kernel(dens, pat_in, wts_in, out, chk, dcol, drow, srow, hop, acc, pat, wts,
+           sums_out, sums_in, parts_out, parts_in, load, send, recv):
     row, col = lax.axis_index("row"), lax.axis_index("col")
     x, yh = row // 2, row % 2
     z, yl, core = col // 4, (col // 2) % 2, col % 2
@@ -156,13 +159,16 @@
     cols_of = [(row, (col + i) % NCOL) for i in range(1, NCOL)]
 
     barrier = pltpu.get_barrier_semaphore()
-    greet = rows_of + cols_of + [peer["yb"]]
+    greet = list(peer.values())
     for device in greet:
         pl.semaphore_signal(barrier, inc=1, device_id=device, device_id_type=MESH)
-
-    tile = dens[...]
-    dcol[row] = tile
-    drow[col] = tile
+    loads = [pltpu.make_async_copy(src, dst, load.at[i]) for i, (src, dst) in enumerate((
+        (pat_in, pat), (wts_in, wts), (dens, drow.at[col]), (dens, dcol.at[row])))]
+    for copy in loads:
+        copy.start()
+    for copy in loads[:2]:
+        copy.wait()
+
     acc[...] = jnp.zeros_like(acc)
     nr, nc = ROWS // BLK, COLS // BLK
     rm = (lax.broadcasted_iota(jnp.int32, (nr, ROWS), 0)
@@ -173,6 +179,8 @@
                    preferred_element_type=jnp.float32)
     mask = jnp.dot(part, rm.astype(jnp.float32), preferred_element_type=jnp.float32)
 
+    for copy in loads[2:]:
+        copy.wait()
     pl.semaphore_wait(barrier, len(greet))
 
     copies = {}
@@ -259,10 +267,10 @@
         return do
 
     plan = Plan()
-    fill_c = ring(plan, "C", PIECES_D, "x+", "x-",
-                  lambda p: ("ya", "yb") if PIECES_D[p][3] > 0 else ("yb", "ya"), column_copy)
-    fill_r = ring(plan, "R", PIECES_D, "z+", "z-", lambda p: ("ya",), panel_copy(drow, colslots))
-    have = mates(plan, "R", drow, fill_r, PIECES_D)
+    fill_c = ring(plan, "C", PIECES_C, "x+", "x-",
+                  lambda p: ("ya", "yb") if PIECES_C[p][3] > 0 else ("yb", "ya"), column_copy)
+    fill_r = ring(plan, "R", PIECES_R, "z+", "z-", lambda p: ("ya",), panel_copy(drow, colslots))
+    have = mates(plan, "R", drow, fill_r, PIECES_R)
 
     def need(r_slots, c_slots):
         return ([n for s in r_slots for n in have[s]] + [n for s in c_slots for n in fill_c[s].values()])
@@ -286,11 +294,10 @@
     plan.add("work3", "work", 2.6, need(near3, near3) + ["work2"], products(drow, stage3))
     plan.run(wait)
 
-    w8 = jnp.broadcast_to(wts[...][None, :], (8, ROWS))
+    w_col = jnp.broadcast_to(wts[...][None, :], (128, ROWS)).T
 
     def column_sums(value):
-        return lax.dot_general(w8, value, (((1,), (1,)), ((), ())),
-                               precision=lax.Precision.HIGHEST, preferred_element_type=jnp.float32)
+        return dot3(value, w_col).T[:8]
 
     srow[col] = mask * acc[...]
 
@@ -302,33 +309,42 @@
         first = lax.broadcasted_iota(jnp.int32, (8, COLS), 0) == 0
         value = jnp.where(first, column_sums(acc[...]), column_sums(srow[col]))
         acc[...] = jnp.zeros_like(acc)
-        sums_out[...] = value
+        sums_out[0] = value
         sums_in[row] = value
         for i, device in enumerate(rows_of):
-            put(f"sums{i}", sums_out, sums_in.at[row], device)
-
-    def parts(_):
+            put(f"sums{i}", sums_out.at[0], sums_in.at[row], device)
+
+    def total_sums(_):
         for i in range(NROW - 1):
             wait(f"sums{i}")
         total = sums_in[0]
         for i in range(1, NROW):
             total += sums_in[i]
         chk[0:1, :] = total[0:1]
-
-        def run(k, carry):
-            value = dot3(total, dcol[k])
-            parts_out[2 * k] = value[:, :COLS]
-            parts_out[2 * k + 1] = value[:, COLS:]
-            return carry
-
-        lax.fori_loop(0, NROW, run, 0)
+        sums_out[1] = total
+
+    def parts(first):
+        def do(_):
+            def run(k, carry):
+                value = dot3(sums_out[1], dcol[k])
+                parts_out[2 * k] = value[:, :COLS]
+                parts_out[2 * k + 1] = value[:, COLS:]
+                return carry
+
+            lax.fori_loop(first, first + 2, run, 0)
+        return do
+
+    def spread(_):
         parts_in[col] = parts_out[col]
         for i, device in enumerate(cols_of):
             put(f"parts{i}", parts_out.at[device[1]], parts_in.at[col], device)
 
     plan.add("sums", "work", 2.5, [], sums)
     plan.add("work0", "work", 1.3, have["mine"] + ["sums"], products(srow, [rowslot(z, yl)]))
-    plan.add("parts", "work", 6.0, fill_s["far"].values(), parts)
+    plan.add("total", "work", 0.3, list(fill_s["back"].values()) + ["work0"], total_sums)
+    for k in range(0, NROW, 2):
+        plan.add(f"parts{k}", "work", 2.0, ["total" if k == 0 else f"parts{k - 2}"], parts(k))
+    plan.add("spread", "work", 0.3, ["parts6"], spread)
     plan.add("work1", "work", 2.6, have["back"] + have["ahead"] + ["work0"],
              products(srow, [rowslot(step(z, 3), yl), rowslot(step(z, 1), yl)]))
     plan.add("work2", "work", 2.6, have["far"] + have["mine_p"] + ["work1"],
@@ -354,10 +370,11 @@
 def body(density, pattern, weights):
     f32 = jnp.float32
     vmem = pl.BlockSpec(memory_space=pltpu.VMEM)
+    hbm = pl.BlockSpec(memory_space=pltpu.HBM)
     purified, checks = pl.pallas_call(
         kernel,
         out_shape=(jax.ShapeDtypeStruct((COLS, ROWS), f32), jax.ShapeDtypeStruct((2, COLS), f32)),
-        in_specs=[vmem] * 3,
+        in_specs=[hbm] * 3,
         out_specs=(vmem, vmem),
         scratch_shapes=[
             pltpu.VMEM((NROW, COLS, ROWS), f32),
@@ -365,17 +382,20 @@
             pltpu.VMEM((NCOL, COLS, ROWS), f32),
             pltpu.VMEM((4, COLS, ROWS), f32),
             pltpu.VMEM((COLS, ROWS), f32),
-            pltpu.VMEM((8, COLS), f32),
+            pltpu.VMEM((COLS // BLK, ROWS // BLK), jnp.int32),
+            pltpu.VMEM((ROWS,), f32),
+            pltpu.VMEM((2, 8, COLS), f32),
             pltpu.VMEM((NROW, 8, COLS), f32),
             pltpu.VMEM((NCOL, 8, COLS), f32),
             pltpu.VMEM((NCOL, 8, COLS), f32),
+            pltpu.SemaphoreType.DMA((4,)),
             pltpu.SemaphoreType.DMA((SEMS,)),
             pltpu.SemaphoreType.DMA((SEMS,)),
         ],
         compiler_params=pltpu.CompilerParams(
-            collective_id=0, has_side_effects=True, vmem_limit_bytes=63 * 1024 * 1024),
+            collective_id=0, has_side_effects=True, vmem_limit_bytes=46 * 1024 * 1024),
         name="purify",
-    )(density.T, pattern.T, weights)
+    )(*(pltpu.with_memory_space_constraint(a, pltpu.HBM) for a in (density.T, pattern.T, weights)))
     return purified.T, checks
 
 

time: 129 us -> 125 us (0.969)
  Pallas kernels: 125 us -> 123 us
    pallas_call x1, Pallas kernels: 125 us -> 123 us  [body(): pl.pallas_call(kernel, out_shape=(jax.ShapeDtypeStruct((COLS, ROWS), f32)...]
    unnamed x4 -> x2, local copies, waits for them, and re-layouts: 2.67 us -> 1.47 us
where the time goes in v4:
time: 125 us
  Pallas kernels  123 us (98%)
  local copies, waits for them, and re-layouts  1.47 us (1%)
    pallas_call x1, Pallas kernels, body(): pl.pallas_call(kernel, out_shape=(jax.ShapeDtypeStruct((COLS, ROWS), f32)...  123 us

profile of v4, /device:TPU:1, one launch (start us, length us, event | category | flops | bytes accessed | tf_op | source)
XLA Modules:
  0.0 125.0 jit_solution(16201307922494549772)
XLA Ops:
  0.6 122.9 %purify.1 = (f32[320,640]{1,0:T(8,128)S(1)}, f32[2,320]{1,0:T(2,128)S(1)}) custom-call(f32[320,640]{1,0:T(8,128)} %bitcast.4, s32[5,10]{1,0:T(8,128)} %bitcast.5, f32[640]{0:T(1024)} %wts_in.1), custom_call_target="tpu_custom_call" | custom-call | tf_op jit(solution)/shard_map/purify/pallas_call | solution.py:374
  123.6 0.9 copy.7
  124.5 0.6 copy.8

commit v5 on v4

--- a/solution.py
+++ b/solution.py
@@ -13,7 +13,7 @@
 
 LINK_ROW, LINK_LATENCY = 0.0545, 1.7
 MATE_ROW, MATE_LATENCY = 0.0057, 1.0
-LEAD = 5.0
+LEAD, PATIENCE, ISSUE = 3.0, 0.5, 0.02
 
 PIECES_C = ((0, 72, "first", 1), (72, 72, "first", 1), (144, 16, "after", 1),
             (160, 72, "first", -1), (232, 72, "first", -1), (304, 16, "after", -1))
@@ -46,25 +46,53 @@
         for name in reversed(list(items)):
             _, length, latency, _, _ = items[name]
             level[name] = length + latency + max([level[n] for n in after[name]], default=0.0)
-        free, there, events = {}, {}, []
-        left = list(items)
+        now, free, there, program = 0.0, {}, {}, []
+        left = sorted(items, key=lambda name: -level[name])
         while left:
-            best = None
+            ready = {}
             for name in left:
-                link, _, _, deps, _ = items[name]
+                deps = items[name][3]
                 if all(dep in there for dep in deps):
-                    ready = max([there[dep] for dep in deps], default=0.0)
-                    key = (max(ready, free.get(link, 0.0)), -level[name], len(events))
-                    if best is None or key < best[0]:
-                        best = (key, name, ready)
-            (start, _, _), name, ready = best
-            link, length, latency, _, _ = items[name]
-            free[link] = start + length
-            there[name] = start + length + latency
-            issue = start if link == "work" else max(ready, start - LEAD)
-            events.append((issue, len(events), name))
-            left.remove(name)
-        return [name for _, _, name in sorted(events)], there
+                    ready[name] = max([there[dep] for dep in deps], default=0.0)
+            chosen, following = None, []
+            for name, since in ready.items():
+                link = items[name][0]
+                if link == "work":
+                    if since > now:
+                        following.append(since)
+                    continue
+                since = max(since, free.get(link, 0.0) - LEAD)
+                if since <= now:
+                    chosen = name
+                    break
+                following.append(since)
+            if chosen is None:
+                for name, since in ready.items():
+                    link, length = items[name][:2]
+                    if link != "work" or since > now:
+                        continue
+                    idle = max([now + length - max(free.get(items[n][0], 0.0), t)
+                                for n, t in ready.items() if items[n][0] not in ("work", "mate")],
+                               default=0.0)
+                    if idle <= PATIENCE:
+                        chosen = name
+                        break
+            if chosen is None:
+                if following:
+                    now = min(following)
+                    continue
+                chosen = next(iter(ready))
+            link, length, latency, _, _ = items[chosen]
+            if link == "work":
+                now += length
+                there[chosen] = now
+            else:
+                free[link] = max(now, free.get(link, 0.0)) + length
+                there[chosen] = free[link] + latency
+                now += ISSUE
+            program.append(chosen)
+            left.remove(chosen)
+        return program, there
 
     def run(self, wait):
         done = set()
@@ -286,12 +314,17 @@
     stage2 = [sel(rowslot(step(x, 2), yl), rowslot(step(x, 1), yl)), rowslot(step(x, 3), yl),
               sel(rowslot(o0, ny), rowslot(step(z, 1), yh)), sel(rowslot(o1, ny), rowslot(step(z, 3), yh))]
     stage3 = [sel(rowslot(o2, ny), rowslot(step(x, 2), yl)), sel(rowslot(o3, ny), rowslot(step(z, 2), yh))]
-    near = ["back", "ahead", "far", "mine_p"]
-    plan.add("work1", "work", 2.6, need(["mine"] + near, near), products(drow, stage1))
-    near2 = near + ["back_p", "ahead_p"]
-    plan.add("work2", "work", 5.2, need(near2, near2) + ["work1"], products(drow, stage2))
-    near3 = near2 + ["far_p"]
-    plan.add("work3", "work", 2.6, need(near3, near3) + ["work2"], products(drow, stage3))
+    own, par = ["back", "ahead", "far"], ["mine_p", "back_p", "ahead_p"]
+    needs = (
+        (["mine"] + own, ["mine_p"]), (["mine"] + own + ["mine_p"], own),
+        (["mine"] + own, ["far", "ahead_p"]), (["mine"] + own, ["back", "back_p"]),
+        (par, own + ["mine_p", "ahead_p"]), (par, own + ["ahead_p", "back_p"]),
+        (["mine"] + own + par + ["far_p"], own + par + ["far_p"]), ([], []),
+    )
+    deps = []
+    for i, (k, slots) in enumerate(zip(stage1 + stage2 + stage3, needs)):
+        deps = deps + need(*slots)
+        plan.add(f"work{i}", "work", 1.3, deps + [f"work{j}" for j in range(i)], products(drow, [k]))
     plan.run(wait)
 
     w_col = jnp.broadcast_to(wts[...][None, :], (128, ROWS)).T
@@ -339,20 +372,16 @@
         for i, device in enumerate(cols_of):
             put(f"parts{i}", parts_out.at[device[1]], parts_in.at[col], device)
 
-    plan.add("sums", "work", 2.5, [], sums)
-    plan.add("work0", "work", 1.3, have["mine"] + ["sums"], products(srow, [rowslot(z, yl)]))
-    plan.add("total", "work", 0.3, list(fill_s["back"].values()) + ["work0"], total_sums)
+    plan.add("sums", "work", 2.0, [], sums)
+    plan.add("total", "work", 0.3, list(fill_s["back"].values()) + ["sums"], total_sums)
     for k in range(0, NROW, 2):
-        plan.add(f"parts{k}", "work", 2.0, ["total" if k == 0 else f"parts{k - 2}"], parts(k))
+        plan.add(f"parts{k}", "work", 1.6, ["total" if k == 0 else f"parts{k - 2}"], parts(k))
     plan.add("spread", "work", 0.3, ["parts6"], spread)
-    plan.add("work1", "work", 2.6, have["back"] + have["ahead"] + ["work0"],
-             products(srow, [rowslot(step(z, 3), yl), rowslot(step(z, 1), yl)]))
-    plan.add("work2", "work", 2.6, have["far"] + have["mine_p"] + ["work1"],
-             products(srow, [rowslot(step(z, 2), yl), rowslot(z, 1 - yl)]))
-    plan.add("work3", "work", 2.6, have["back_p"] + have["ahead_p"] + ["work2"],
-             products(srow, [rowslot(step(z, 3), 1 - yl), rowslot(step(z, 1), 1 - yl)]))
-    plan.add("work4", "work", 1.3, have["far_p"] + ["work3"],
-             products(srow, [rowslot(step(z, 2), 1 - yl)]))
+    blocks = {"mine": (0, yl), "back": (3, yl), "ahead": (1, yl), "far": (2, yl)}
+    blocks |= {f"{slot}_p": (by, 1 - y) for slot, (by, y) in blocks.items()}
+    for slot, (by, y) in blocks.items():
+        plan.add(f"work_{slot}", "work", 1.3, have[slot] + ["sums"],
+                 products(srow, [rowslot(step(z, by), y)]))
     plan.run(wait)
 
     out[...] = 3.0 * srow[col] - 2.0 * (mask * acc[...])

time: 125 us -> 119 us (0.952)
  Pallas kernels: 123 us -> 117 us
    pallas_call x1, Pallas kernels: 123 us -> 117 us  [body(): pl.pallas_call(kernel, out_shape=(jax.ShapeDtypeStruct((COLS, ROWS), f32)...]
where the time goes in v5:
time: 119 us
  Pallas kernels  117 us (98%)
  local copies, waits for them, and re-layouts  1.47 us (1%)
    pallas_call x1, Pallas kernels, body(): pl.pallas_call(kernel, out_shape=(jax.ShapeDtypeStruct((COLS, ROWS), f32)...  117 us

profile of v5, /device:TPU:1, one launch (start us, length us, event | category | flops | bytes accessed | tf_op | source)
XLA Modules:
  0.0 118.8 jit_solution(9878509284217022110)
XLA Ops:
  0.6 116.7 %purify.1 = (f32[320,640]{1,0:T(8,128)S(1)}, f32[2,320]{1,0:T(2,128)S(1)}) custom-call(f32[320,640]{1,0:T(8,128)} %bitcast.4, s32[5,10]{1,0:T(8,128)} %bitcast.5, f32[640]{0:T(1024)} %wts_in.1), custom_call_target="tpu_custom_call" | custom-call | tf_op jit(solution)/shard_map/purify/pallas_call | solution.py:403
  117.4 0.9 copy.7
  118.3 0.6 copy.8

commit v6 on v5

--- a/solution.py
+++ b/solution.py
@@ -11,7 +11,7 @@
 NROW, NCOL = 8, 16
 SEMS = 240
 
-LINK_ROW, LINK_LATENCY = 0.0545, 1.7
+LINK_ROW, LINK_LATENCY = 0.0545, 3.0
 MATE_ROW, MATE_LATENCY = 0.0057, 1.0
 LEAD, PATIENCE, ISSUE = 3.0, 0.5, 0.02
 
@@ -108,7 +108,7 @@
                 wait(name)
 
 
-def ring(plan, tag, pieces, plus, minus, cross, send_to):
+def ring(plan, tag, pieces, plus, minus, cross, send_to, start=lambda p: []):
     fills = {slot: {} for slot in ("back", "ahead", "far", "mine_p", "back_p", "ahead_p", "far_p")}
 
     def over(name, src, dst, p, deps):
@@ -136,12 +136,12 @@
         fills[far][p] = name
 
     for p, (first, rows, when, way) in enumerate(pieces):
-        around("own", p, [], ("mine", "back", "ahead", "far"))
+        around("own", p, start(p), ("mine", "back", "ahead", "far"))
         if when == "first":
-            last = over(f"{tag}y{p}", "mine", "mine_p", p, [])
+            last = over(f"{tag}y{p}", "mine", "mine_p", p, start(p))
             around("par", p, last, ("mine_p", "back_p", "ahead_p", "far_p"))
         else:
-            over(f"{tag}y{p}", "mine", "mine_p", p, [])
+            over(f"{tag}y{p}", "mine", "mine_p", p, start(p))
             for slot in ("back", "ahead", "far"):
                 over(f"{tag}y{slot}{p}", slot, slot + "_p", p, [fills[slot][p]])
     return fills
@@ -206,6 +206,11 @@
     part = jnp.dot(cm.astype(jnp.float32), pat[...].astype(jnp.float32),
                    preferred_element_type=jnp.float32)
     mask = jnp.dot(part, rm.astype(jnp.float32), preferred_element_type=jnp.float32)
+
+    w_col = jnp.broadcast_to(wts[...][None, :], (128, ROWS)).T
+
+    def column_sums(value):
+        return dot3(value, w_col).T[:8]
 
     for copy in loads[2:]:
         copy.wait()
@@ -255,12 +260,13 @@
         there = dcol.at[origin, span, :]
         return lambda _: put(name, between, there, peer[link])
 
-    def mates(plan, tag, buf, fills, pieces):
+    def mates(tag, buf, fills, pieces, start=lambda half: []):
         given = {"mine": []}
-        name = f"{tag}m"
-        ref = buf.at[col]
-        plan.add(name, "mate", COLS, [], lambda _, n=name, r=ref: put(n, r, r, peer["mate"]))
-        given["mine"].append(name)
+        for half, (first, rows) in enumerate(GROUPS):
+            name = f"{tag}m{first}"
+            ref = buf.at[col, pl.ds(first, rows), :]
+            plan.add(name, "mate", rows, start(half), lambda _, n=name, r=ref: put(n, r, r, peer["mate"]))
+            given["mine"].append(name)
         for slot, by in fills.items():
             given[slot] = []
             groups = [q[:2] for q in pieces] if slot == "far_p" else GROUPS
@@ -272,33 +278,17 @@
                 given[slot].append(name)
         return {slot: list(by.values()) + given[slot] for slot, by in fills.items()} | {"mine": given["mine"]}
 
-    def product(panel, k):
-        acc[...] += dot3(dcol[k], panel[pl.ds(2 * k, 2)].reshape(2 * COLS, ROWS))
-
-    def pick(i, values):
-        k = values[-1]
-        for j in reversed(range(len(values) - 1)):
-            k = jnp.where(i == j, values[j], k)
-        return k
-
-    def products(panel, ks):
+    def product(panel, k, which, first=0, rows=COLS):
         def do(_):
-            if len(ks) == 1:
-                product(panel, ks[0])
-                return
-
-            def run(i, carry):
-                product(panel, pick(i, ks))
-                return carry
-
-            lax.fori_loop(0, len(ks), run, 0)
+            span = pl.ds(first, rows)
+            acc[which, span, :] += dot3(dcol[k, span, :], panel[pl.ds(2 * k, 2)].reshape(2 * COLS, ROWS))
         return do
 
     plan = Plan()
     fill_c = ring(plan, "C", PIECES_C, "x+", "x-",
                   lambda p: ("ya", "yb") if PIECES_C[p][3] > 0 else ("yb", "ya"), column_copy)
     fill_r = ring(plan, "R", PIECES_R, "z+", "z-", lambda p: ("ya",), panel_copy(drow, colslots))
-    have = mates(plan, "R", drow, fill_r, PIECES_R)
+    have = mates("R", drow, fill_r, PIECES_R)
 
     def need(r_slots, c_slots):
         return ([n for s in r_slots for n in have[s]] + [n for s in c_slots for n in fill_c[s].values()])
@@ -322,26 +312,36 @@
         (["mine"] + own + par + ["far_p"], own + par + ["far_p"]), ([], []),
     )
     deps = []
-    for i, (k, slots) in enumerate(zip(stage1 + stage2 + stage3, needs)):
+    blocks = stage1 + stage2 + stage3
+    for i, (k, slots) in enumerate(zip(blocks[:6], needs)):
         deps = deps + need(*slots)
-        plan.add(f"work{i}", "work", 1.3, deps + [f"work{j}" for j in range(i)], products(drow, [k]))
-    plan.run(wait)
-
-    w_col = jnp.broadcast_to(wts[...][None, :], (128, ROWS)).T
-
-    def column_sums(value):
-        return dot3(value, w_col).T[:8]
-
-    srow[col] = mask * acc[...]
-
-    plan = Plan()
-    fill_s = ring(plan, "S", PIECES_S, "z+", "z-", lambda p: ("ya",), panel_copy(srow, colslots))
-    have = mates(plan, "S", srow, fill_s, PIECES_S)
+        plan.add(f"work{i}", "work", 1.3, deps, product(drow, k, 0))
+        deps = deps + [f"work{i}"]
+    deps = deps + need(*needs[6])
+
+    def square(first, rows):
+        def do(_):
+            span = pl.ds(first, rows)
+            srow[col, span, :] = mask[first:first + rows] * acc[0, span, :]
+        return do
+
+    for half, (first, rows) in enumerate(GROUPS):
+        for i in (6, 7):
+            plan.add(f"work{i}/{half}", "work", 0.75, deps, product(drow, blocks[i], 0, first, rows))
+            deps = deps + [f"work{i}/{half}"]
+        plan.add(f"square{half}", "work", 0.4, deps, square(first, rows))
+        deps = deps + [f"square{half}"]
+
+    def squared(half):
+        return [f"square{half}"]
+
+    fill_s = ring(plan, "S", PIECES_S, "z+", "z-", lambda p: ("ya",), panel_copy(srow, colslots),
+                  lambda p: squared(PIECES_S[p][0] // GROUPS[0][1]))
+    have = mates("S", srow, fill_s, PIECES_S, squared)
 
     def sums(_):
         first = lax.broadcasted_iota(jnp.int32, (8, COLS), 0) == 0
-        value = jnp.where(first, column_sums(acc[...]), column_sums(srow[col]))
-        acc[...] = jnp.zeros_like(acc)
+        value = jnp.where(first, column_sums(acc[0]), column_sums(srow[col]))
         sums_out[0] = value
         sums_in[row] = value
         for i, device in enumerate(rows_of):
@@ -372,19 +372,19 @@
         for i, device in enumerate(cols_of):
             put(f"parts{i}", parts_out.at[device[1]], parts_in.at[col], device)
 
-    plan.add("sums", "work", 2.0, [], sums)
+    plan.add("sums", "work", 2.0, ["square1"], sums)
     plan.add("total", "work", 0.3, list(fill_s["back"].values()) + ["sums"], total_sums)
     for k in range(0, NROW, 2):
         plan.add(f"parts{k}", "work", 1.6, ["total" if k == 0 else f"parts{k - 2}"], parts(k))
     plan.add("spread", "work", 0.3, ["parts6"], spread)
-    blocks = {"mine": (0, yl), "back": (3, yl), "ahead": (1, yl), "far": (2, yl)}
-    blocks |= {f"{slot}_p": (by, 1 - y) for slot, (by, y) in blocks.items()}
-    for slot, (by, y) in blocks.items():
-        plan.add(f"work_{slot}", "work", 1.3, have[slot] + ["sums"],
-                 products(srow, [rowslot(step(z, by), y)]))
+    places = {"mine": (0, yl), "back": (3, yl), "ahead": (1, yl), "far": (2, yl)}
+    places |= {f"{slot}_p": (by, 1 - y) for slot, (by, y) in places.items()}
+    for slot, (by, y) in places.items():
+        plan.add(f"work_{slot}", "work", 1.3, have[slot] + ["square1"],
+                 product(srow, rowslot(step(z, by), y), 1))
     plan.run(wait)
 
-    out[...] = 3.0 * srow[col] - 2.0 * (mask * acc[...])
+    out[...] = 3.0 * srow[col] - 2.0 * (mask * acc[1])
     for i in range(NCOL - 1):
         wait(f"parts{i}")
     total = parts_in[0]
@@ -410,7 +410,7 @@
             pltpu.VMEM((NCOL, COLS, ROWS), f32),
             pltpu.VMEM((NCOL, COLS, ROWS), f32),
             pltpu.VMEM((4, COLS, ROWS), f32),
-            pltpu.VMEM((COLS, ROWS), f32),
+            pltpu.VMEM((2, COLS, ROWS), f32),
             pltpu.VMEM((COLS // BLK, ROWS // BLK), jnp.int32),
             pltpu.VMEM((ROWS,), f32),
             pltpu.VMEM((2, 8, COLS), f32),

time: 119 us -> 116 us (0.975)
  Pallas kernels: 117 us -> 113 us
    pallas_call x1, Pallas kernels: 117 us -> 113 us  [body(): pl.pallas_call(kernel, out_shape=(jax.ShapeDtypeStruct((COLS, ROWS), f32)...]
where the time goes in v6:
time: 116 us; the launch traced here: 115 us
  Pallas kernels  113 us (97%)
  local copies, waits for them, and re-layouts  1.47 us (1%)
    pallas_call x1, Pallas kernels, body(): pl.pallas_call(kernel, out_shape=(jax.ShapeDtypeStruct((COLS, ROWS), f32)...  113 us

profile of v6, /device:TPU:1, one launch (start us, length us, event | category | flops | bytes accessed | tf_op | source)
XLA Modules:
  0.0 115.4 jit_solution(9470234345007771659)
XLA Ops:
  0.6 113.3 %purify.1 = (f32[320,640]{1,0:T(8,128)S(1)}, f32[2,320]{1,0:T(2,128)S(1)}) custom-call(f32[320,640]{1,0:T(8,128)} %bitcast.4, s32[5,10]{1,0:T(8,128)} %bitcast.5, f32[640]{0:T(1024)} %wts_in.1), custom_call_target="tpu_custom_call" | custom-call | tf_op jit(solution)/shard_map/purify/pallas_call | solution.py:403
  113.9 0.9 copy.7
  114.8 0.6 copy.8

commit v7 on v6

--- a/solution.py
+++ b/solution.py
@@ -15,10 +15,10 @@
 MATE_ROW, MATE_LATENCY = 0.0057, 1.0
 LEAD, PATIENCE, ISSUE = 3.0, 0.5, 0.02
 
-PIECES_C = ((0, 72, "first", 1), (72, 72, "first", 1), (144, 16, "after", 1),
-            (160, 72, "first", -1), (232, 72, "first", -1), (304, 16, "after", -1))
-PIECES_R = ((0, 64, "first", 1), (64, 72, "first", 1), (136, 24, "after", 1),
-            (160, 64, "first", -1), (224, 72, "first", -1), (296, 24, "after", -1))
+PIECES_C = ((0, 16, "after", 1), (16, 48, "first", 1), (64, 96, "first", 1),
+            (160, 16, "after", -1), (176, 48, "first", -1), (224, 96, "first", -1))
+PIECES_R = ((0, 32, "first", 1), (32, 32, "first", 1), (64, 72, "first", 1), (136, 24, "after", 1),
+            (160, 32, "first", -1), (192, 32, "first", -1), (224, 72, "first", -1), (296, 24, "after", -1))
 PIECES_S = ((0, 88, "first", 1), (88, 72, "after", 1), (160, 88, "first", -1), (248, 72, "after", -1))
 GROUPS = ((0, 160), (160, 160))
 

time: 116 us -> 115 us (level)
  no operation moved by 1% of the time
where the time goes in v7:
time: 115 us
  Pallas kernels  113 us (98%)
  local copies, waits for them, and re-layouts  1.47 us (1%)
    pallas_call x1, Pallas kernels, body(): pl.pallas_call(kernel, out_shape=(jax.ShapeDtypeStruct((COLS, ROWS), f32)...  113 us

profile of v7, /device:TPU:1, one launch (start us, length us, event | category | flops | bytes accessed | tf_op | source)
XLA Modules:
  0.0 114.8 jit_solution(6176513636882146358)
XLA Ops:
  0.6 112.7 %purify.1 = (f32[320,640]{1,0:T(8,128)S(1)}, f32[2,320]{1,0:T(2,128)S(1)}) custom-call(f32[320,640]{1,0:T(8,128)} %bitcast.4, s32[5,10]{1,0:T(8,128)} %bitcast.5, f32[640]{0:T(1024)} %wts_in.1), custom_call_target="tpu_custom_call" | custom-call | tf_op jit(solution)/shard_map/purify/pallas_call | solution.py:403
  113.3 0.9 copy.7
  114.2 0.6 copy.8
